TPU v7x, 32 devices: a whole 2x2x4 slice. The times are simulated.
32 devices in a mesh: dp: 8 (over z, x), mp: 4 (over y, core).
Axes of the slice: x: 2, y: 2, z: 4, core: 2. Of those that a mesh axis runs over, the one named last changes fastest.
Arguments:
- tokens_in: bfloat16 [8, 1024, 2048], P('dp'), may hold values from -6 to 6
- cotangent: bfloat16 [8, 1024, 2048], P('dp'), may hold values from -6 to 6
- select_mask: int32 [8, 1024], P('dp'), may hold values 0 or 1
- doc_ids: int32 [8, 1024], P('dp'), may hold values from 0 to 3, never falling along the last dimension, each value on 1 to 512 neighbouring positions
- norm_gains: float32 [2, 2048], replicated, may hold values from 0.5 to 1.5
- weight_blocks: float32 [2688, 128, 128], P(('dp', 'mp'))
- ema_blocks: float32 [2688, 128, 128], P(('dp', 'mp')), may hold values from -1.5 to 1.5
- left_stats: float32 [2688, 128, 128], P(('dp', 'mp')), as said below
- right_stats: float32 [2688, 128, 128], P(('dp', 'mp')), as said below
- left_roots: float32 [2688, 128, 128], P(('dp', 'mp')), as said below
- right_roots: float32 [2688, 128, 128], P(('dp', 'mp')), as said below
Outputs:
- block_out: bfloat16 [8, 1024, 2048], P('dp')
- input_grad: float32 [8, 1024, 2048], P('dp')
- block_grads: float32 [2688, 128, 128], P(('dp', 'mp'))
- new_weights: float32 [2688, 128, 128], P(('dp', 'mp'))
- new_ema: float32 [2688, 128, 128], P(('dp', 'mp'))
- new_left: float32 [2688, 128, 128], P(('dp', 'mp'))
- new_right: float32 [2688, 128, 128], P(('dp', 'mp'))
- gain_grads: float32 [2, 2048], P(None, 'dp')
- new_gains: float32 [2, 2048], P(None, 'dp')
Inputs may be any that keep to these rules, and one draw needn't show every extreme that they name: `doc_ids`: within each sequence the ids never fall; every one of the 4 documents has 1 to 512 positions. `left_stats`: each block is symmetric. `right_stats`: each block is symmetric. `left_roots`: each block is symmetric. `right_roots`: each block is symmetric.
All inputs are finite; a program needn't handle non-finite values. No bound on the sum of `select_mask` on one device may be relied on, other than what follows from the above.
Results may differ from a plain program's by a relative error of at most 0.015.
The roundings to bfloat16 on the way count: a program that leaves them out, or rounds other values in their place, can miss the bound.
Values may be sent and summed in bfloat16 or wider, within the bound.
No kernel may reach another device: no remote copies, remote signals or barrier semaphores. Data moves between devices by JAX's collectives and lax.ppermute only.
A program may use at most 320 MiB of HBM per device.

v0:
```python
import jax
import jax.numpy as jnp
from jax import lax
from jax.sharding import PartitionSpec as P

HEADS = 32
KV_HEADS = 4
HD = 64
FF = 5632
highest = lax.Precision.HIGHEST
weight_rate = 1.0
gain_rate = 0.2
average_decay = 0.9


def doc_positions(doc_ids):
    length = doc_ids.shape[-1]
    offsets = jnp.arange(length, dtype=jnp.int32)
    starts = jnp.concatenate(
        [jnp.ones(doc_ids.shape[:-1] + (1,), jnp.bool_), doc_ids[..., 1:] != doc_ids[..., :-1]],
        axis=-1,
    )
    first_index = lax.cummax(jnp.where(starts, offsets, 0), axis=doc_ids.ndim - 1)
    return offsets - first_index


def rope_tables(positions, head_size):
    half_size = head_size // 2
    exponent = jnp.arange(half_size, dtype=jnp.float32) * (2.0 / head_size)
    inverse = jnp.power(jnp.float32(10000.0), -exponent)
    angles = positions.astype(jnp.float32)[..., None] * inverse
    return (jnp.cos(angles), jnp.sin(angles))


def rotate(values, cosine_table, sine_table):
    half_size = values.shape[-1] // 2
    first_half = values[..., :half_size]
    second_half = values[..., half_size:]
    return jnp.concatenate(
        [
            first_half * cosine_table - second_half * sine_table,
            second_half * cosine_table + first_half * sine_table,
        ],
        axis=-1,
    )


def rotate_back(grads, cosine_table, sine_table):
    half_size = grads.shape[-1] // 2
    first_half = grads[..., :half_size]
    second_half = grads[..., half_size:]
    return jnp.concatenate(
        [
            first_half * cosine_table + second_half * sine_table,
            second_half * cosine_table - first_half * sine_table,
        ],
        axis=-1,
    )


def normalize(values, gain):
    inverse_rms = lax.rsqrt(jnp.mean(values * values, axis=-1, keepdims=True) + 1e-05)
    unit = values * inverse_rms
    return (unit * gain, unit, inverse_rms)


def normalize_back(grad_out, unit, inverse_rms, gain):
    scaled = grad_out * gain
    return inverse_rms * (scaled - unit * jnp.mean(scaled * unit, axis=-1, keepdims=True))


def project(inputs, weights):
    row_count = inputs.shape[0]
    shaped = inputs.reshape(row_count, weights.shape[0], weights.shape[-1])
    return jnp.einsum("tri,rcij->tcj", shaped, weights, preferred_element_type=jnp.float32).reshape(
        row_count, -1
    )


def project_back(grads, weights):
    row_count = grads.shape[0]
    shaped = grads.reshape(row_count, weights.shape[1], weights.shape[-1])
    return jnp.einsum("tcj,rcij->tri", shaped, weights, preferred_element_type=jnp.float32).reshape(
        row_count, -1
    )


def weight_grad(inputs, grads, block_size):
    row_count = inputs.shape[0]
    left_shaped = inputs.reshape(row_count, -1, block_size)
    right_shaped = grads.reshape(row_count, -1, block_size)
    return jnp.einsum(
        "tri,tcj->rcij", left_shaped, right_shaped, preferred_element_type=jnp.float32
    )


def split_weights(gathered, row_blocks, attn_blocks, in_blocks, out_attn_blocks):
    block_size = gathered.shape[-1]
    in_count = row_blocks * in_blocks
    w_input = gathered[:in_count].reshape(row_blocks, in_blocks, block_size, block_size)
    w_output = gathered[in_count:].reshape(-1, row_blocks, block_size, block_size)
    return (
        w_input[:, :attn_blocks],
        w_input[:, attn_blocks:],
        w_output[:out_attn_blocks],
        w_output[out_attn_blocks:],
    )


def block_scores(query_part, keys, doc_ids, offset, scale):
    row_count = query_part.shape[0]
    query_index = offset + jnp.arange(row_count)
    key_index = jnp.arange(keys.shape[0])
    allowed = (key_index[None, :] <= query_index[:, None]) & (
        doc_ids[None, :] == doc_ids[offset : offset + row_count][:, None]
    )
    scores = (
        jnp.einsum("qgjd,kgd->gjqk", query_part, keys, preferred_element_type=jnp.float32) * scale
    )
    return jnp.where(allowed, scores, -1e30)


def attend_forward(queries, keys, values, doc_ids, query_block):
    length = queries.shape[0]
    scale = float(queries.shape[-1]) ** (-0.5)
    outputs = []
    totals = []
    for offset in range(0, length, query_block):
        scores = block_scores(queries[offset : offset + query_block], keys, doc_ids, offset, scale)
        maximum = jnp.max(scores, axis=-1, keepdims=True)
        expo_values = jnp.exp(scores - maximum)
        denominator = jnp.sum(expo_values, axis=-1, keepdims=True)
        probs = (expo_values / denominator).astype(jnp.bfloat16)
        outputs.append(
            jnp.einsum("gjqk,kgd->qgjd", probs, values, preferred_element_type=jnp.float32)
        )
        totals.append(maximum + jnp.log(denominator))
    return (jnp.concatenate(outputs, axis=0), jnp.concatenate(totals, axis=2))


def attend_backward(queries, keys, values, doc_ids, log_totals, out_grads, query_block):
    length = queries.shape[0]
    scale = float(queries.shape[-1]) ** (-0.5)
    key_grads = jnp.zeros(keys.shape, jnp.float32)
    value_grads = jnp.zeros(values.shape, jnp.float32)
    query_grads = []
    for offset in range(0, length, query_block):
        query_part = queries[offset : offset + query_block]
        scores = block_scores(query_part, keys, doc_ids, offset, scale)
        probs = jnp.exp(scores - log_totals[:, :, offset : offset + query_block])
        grad_part = out_grads[offset : offset + query_block]
        value_grads = value_grads + jnp.einsum(
            "gjqk,qgjd->kgd",
            probs.astype(jnp.bfloat16),
            grad_part,
            preferred_element_type=jnp.float32,
        )
        prob_grads = jnp.einsum(
            "qgjd,kgd->gjqk", grad_part, values, preferred_element_type=jnp.float32
        )
        inner = jnp.sum(probs * prob_grads, axis=-1, keepdims=True)
        score_grads = (probs * (prob_grads - inner)).astype(jnp.bfloat16)
        query_grads.append(
            jnp.einsum("gjqk,kgd->qgjd", score_grads, keys, preferred_element_type=jnp.float32)
            * scale
        )
        key_grads = (
            key_grads
            + jnp.einsum(
                "gjqk,qgjd->kgd", score_grads, query_part, preferred_element_type=jnp.float32
            )
            * scale
        )
    return (jnp.concatenate(query_grads, axis=0), key_grads, value_grads)


def ring_order(count):
    return list(range(0, count, 2)) + list(range(1, count, 2))[::-1]


def sum_rows(values):
    return lax.psum_scatter(
        values.astype(jnp.bfloat16), "mp", scatter_dimension=0, tiled=True
    ).astype(jnp.float32)


def on_device(
    tokens_in,
    cotangent,
    select_mask,
    doc_ids,
    norm_gains,
    weight_blocks,
    ema_blocks,
    left_stats,
    right_stats,
    left_roots,
    right_roots,
):
    mp_count = lax.axis_size("mp")
    dp_count = lax.axis_size("dp")
    sequences, length, model_width = tokens_in.shape
    row_count = sequences * length
    block_size = weight_blocks.shape[-1]
    query_cols = HEADS * HD // mp_count
    key_cols = KV_HEADS * HD // mp_count
    hidden_cols = FF // mp_count
    kv_local = KV_HEADS // mp_count
    group_size = HEADS // KV_HEADS
    row_blocks = model_width // block_size
    attn_blocks = (query_cols + 2 * key_cols) // block_size
    in_blocks = attn_blocks + 2 * hidden_cols // block_size
    out_attn_blocks = query_cols // block_size
    query_block = min(512, length)
    share_rows = row_count // mp_count
    share_start = lax.axis_index("mp") * share_rows

    def row_share(values):
        return lax.dynamic_slice_in_dim(values, share_start, share_rows, 0)

    ring = ring_order(dp_count)
    places = [ring.index(rank) for rank in range(dp_count)]
    own = weight_blocks.shape[0]
    weights_low = weight_blocks.astype(jnp.bfloat16)
    in_ring = lax.all_gather(weights_low, "dp", axis=0, tiled=True, axis_index_groups=[ring])
    gathered = jnp.concatenate(
        [in_ring[place * own : (place + 1) * own] for place in places], axis=0
    )
    w_qkv, w_gateup, w_attn_out, w_down = split_weights(
        gathered, row_blocks, attn_blocks, in_blocks, out_attn_blocks
    )
    positions = doc_positions(doc_ids)
    cosine_table, sine_table = rope_tables(positions, HD)
    query_cos = cosine_table[:, :, None, None, :]
    query_sin = sine_table[:, :, None, None, :]
    key_cos = cosine_table[:, :, None, :]
    key_sin = sine_table[:, :, None, :]
    tokens = tokens_in.astype(jnp.float32).reshape(row_count, model_width)
    first_norm, first_unit, first_scale = normalize(tokens, norm_gains[0])
    first_in = first_norm.astype(jnp.bfloat16)
    qkv = project(first_in, w_qkv)
    queries_raw = qkv[:, :query_cols].reshape(sequences, length, kv_local, group_size, HD)
    keys_raw = qkv[:, query_cols : query_cols + key_cols].reshape(sequences, length, kv_local, HD)
    values_raw = qkv[:, query_cols + key_cols :].reshape(sequences, length, kv_local, HD)
    query_use = rotate(queries_raw, query_cos, query_sin).astype(jnp.bfloat16)
    key_use = rotate(keys_raw, key_cos, key_sin).astype(jnp.bfloat16)
    value_use = values_raw.astype(jnp.bfloat16)

    def forward_one(items):
        return attend_forward(items[0], items[1], items[2], items[3], query_block)

    mixed, log_totals = lax.map(forward_one, (query_use, key_use, value_use, doc_ids))
    mixed_use = mixed.reshape(row_count, query_cols).astype(jnp.bfloat16)
    attended_part = sum_rows(project(mixed_use, w_attn_out))
    middle = row_share(tokens) + attended_part
    second_norm, second_unit, second_scale = normalize(middle, norm_gains[1])
    second_in = lax.all_gather(second_norm.astype(jnp.bfloat16), "mp", axis=0, tiled=True)
    gateup = project(second_in, w_gateup)
    gate = gateup[:, :hidden_cols]
    up_part = gateup[:, hidden_cols:]
    sigmoid_gate = jax.nn.sigmoid(gate)
    hidden = (gate * sigmoid_gate * up_part).astype(jnp.bfloat16)
    feed_part = sum_rows(project(hidden, w_down))
    out_whole = lax.all_gather((middle + feed_part).astype(jnp.bfloat16), "mp", axis=0, tiled=True)
    block_out = out_whole.reshape(sequences, length, model_width)
    out_grad = cotangent.astype(jnp.float32).reshape(row_count, model_width) * select_mask.astype(
        jnp.float32
    ).reshape(row_count, 1)
    mlp_grad = out_grad.astype(jnp.bfloat16)
    grad_down = weight_grad(hidden, mlp_grad, block_size)
    hidden_grad = project_back(mlp_grad, w_down)
    gate_grad = hidden_grad * up_part * sigmoid_gate * (1.0 + gate * (1.0 - sigmoid_gate))
    up_grad = hidden_grad * gate * sigmoid_gate
    gateup_grad = jnp.concatenate([gate_grad, up_grad], axis=1).astype(jnp.bfloat16)
    grad_gateup = weight_grad(second_in, gateup_grad, block_size)
    second_grad = sum_rows(project_back(gateup_grad, w_gateup))
    middle_grad = row_share(out_grad) + normalize_back(
        second_grad, second_unit, second_scale, norm_gains[1]
    )
    second_gain = jnp.sum(second_grad * second_unit, axis=0)
    attn_grad = lax.all_gather(middle_grad.astype(jnp.bfloat16), "mp", axis=0, tiled=True)
    grad_attn_out = weight_grad(mixed_use, attn_grad, block_size)
    mixed_grad = (
        project_back(attn_grad, w_attn_out)
        .astype(jnp.bfloat16)
        .reshape(sequences, length, kv_local, group_size, HD)
    )

    def backward_one(items):
        return attend_backward(
            items[0], items[1], items[2], items[3], items[4], items[5], query_block
        )

    query_grad, key_grad, value_grad = lax.map(
        backward_one, (query_use, key_use, value_use, doc_ids, log_totals, mixed_grad)
    )
    query_grad = rotate_back(query_grad, query_cos, query_sin).reshape(row_count, query_cols)
    key_grad = rotate_back(key_grad, key_cos, key_sin).reshape(row_count, key_cols)
    qkv_grad = jnp.concatenate(
        [query_grad, key_grad, value_grad.reshape(row_count, key_cols)], axis=1
    ).astype(jnp.bfloat16)
    grad_qkv = weight_grad(first_in, qkv_grad, block_size)
    first_grad = sum_rows(project_back(qkv_grad, w_qkv))
    unit_share = row_share(first_unit)
    input_part = middle_grad + normalize_back(
        first_grad, unit_share, row_share(first_scale), norm_gains[0]
    )
    first_gain = jnp.sum(first_grad * unit_share, axis=0)
    gain_part = jnp.stack([first_gain, second_gain], axis=0)
    input_grad, gain_rows = (
        lax.all_gather(input_part.astype(jnp.bfloat16), "mp", axis=0, tiled=True).astype(
            jnp.float32
        ),
        lax.all_gather(gain_part, "mp", axis=0, tiled=True),
    )
    gain_terms = jnp.sum(gain_rows.reshape(mp_count, 2, model_width), axis=0)
    in_grads = jnp.concatenate([grad_qkv, grad_gateup], axis=1).reshape(-1, block_size, block_size)
    out_grads = jnp.concatenate([grad_attn_out, grad_down], axis=0).reshape(
        -1, block_size, block_size
    )
    all_grads = jnp.concatenate([in_grads, out_grads], axis=0).astype(jnp.bfloat16)
    reduced, gain_sums = (
        lax.psum_scatter(
            jnp.concatenate([all_grads[rank * own : (rank + 1) * own] for rank in ring], axis=0),
            "dp",
            scatter_dimension=0,
            tiled=True,
            axis_index_groups=[ring],
        ).astype(jnp.float32),
        lax.psum_scatter(gain_terms, "dp", scatter_dimension=1, tiled=True),
    )
    factor = float(row_count * dp_count) ** (-0.5)
    grads = reduced * factor
    gain_grads = gain_sums * factor
    new_left = 0.5 * left_stats + 0.5 * jnp.einsum("bij,bkj->bik", grads, grads, precision=highest)
    new_right = 0.5 * right_stats + 0.5 * jnp.einsum(
        "bji,bjk->bik", grads, grads, precision=highest
    )
    right_part = jnp.einsum("bij,bjk->bik", grads, right_roots, precision=highest)
    direction = jnp.einsum("bij,bjk->bik", left_roots, right_part, precision=highest)
    new_weights = weight_blocks - weight_rate * direction
    new_ema = average_decay * ema_blocks + (1.0 - average_decay) * new_weights
    share = model_width // dp_count
    gain_share = lax.dynamic_slice_in_dim(norm_gains, lax.axis_index("dp") * share, share, 1)
    new_gains = gain_share - gain_rate * gain_grads
    input_out = input_grad.reshape(sequences, length, model_width)
    return (
        block_out,
        input_out,
        grads,
        new_weights,
        new_ema,
        new_left,
        new_right,
        gain_grads,
        new_gains,
    )


def solution(mesh):
    in_specs = (
        P("dp", None, None),
        P("dp", None, None),
        P("dp", None),
        P("dp", None),
        P(),
        P(("dp", "mp"), None, None),
        P(("dp", "mp"), None, None),
        P(("dp", "mp"), None, None),
        P(("dp", "mp"), None, None),
        P(("dp", "mp"), None, None),
        P(("dp", "mp"), None, None),
    )
    out_specs = (
        P("dp", None, None),
        P("dp", None, None),
        P(("dp", "mp"), None, None),
        P(("dp", "mp"), None, None),
        P(("dp", "mp"), None, None),
        P(("dp", "mp"), None, None),
        P(("dp", "mp"), None, None),
        P(None, "dp"),
        P(None, "dp"),
    )
    return jax.shard_map(
        on_device, mesh=mesh, in_specs=in_specs, out_specs=out_specs, check_vma=False
    )
```

profile of v0, /device:TPU:0, one launch (start us, length us, event | category | flops | bytes accessed | tf_op | source)
XLA Modules:
  0.0 1200.5 jit_solution(14629774651332840294)
XLA Ops:
  7.2 4.7 convert_element_type.160
  12.0 14.3 %convert_bitcast_fusion.2 = (f32[1024,2048]{1,0:T(8,128)}, f32[128,8,16,128]{3,1,2,0:T(8,128)}, f32[1,1024,2048]{2,1,0:T(8,128)}) fusion(bf16[1,1024,2048]{2,1,0:T(8,128)(2,1)} %param.11), kind=kLoop, calls=%fused_computation.50 | loop fusion | flops 2097152 | bytes 29360128 | tf_op jit(solution)/shard_map/reshape | solution.py:238
  26.3 8.7 copy.178
  41.2 188.6 %all-gather.7.cloned.1.call-done = bf16[672,128,128]{2,1,0:T(8,128)(2,1)} async-done(((bf16[84,128,128]{2,1,0:T(8,128)(2,1)}), bf16[672,128,128]{2,1,0:T(8,128)(2,1)}) %all-gather.7.cloned.1.call-update) | async-done | bytes 22020112 | tf_op jit(solution)/shard_map/all_gather | solution.py:225
  229.8 3.9 slice_dynamic-update-slice_fusion.10
  233.6 4.4 slice_dynamic-update-slice_fusion.9
  238.0 4.4 slice_dynamic-update-slice_fusion.8
  249.8 3.8 fusion.144
  253.6 7.7 slice.234
  261.3 5.0 copy-done.1
  271.6 9.0 fusion.76
  282.1 7.2 fusion.148
  289.2 8.0 fusion.7
  297.3 7.4 fusion.86
  304.8 7.6 fusion.149
  312.4 8.2 fusion.6
  320.7 9.0 fusion.83
  336.0 4.4 bitcast_convert_fusion.3
  340.5 44.6 %reduce-scatter.9.cloned.1.call-done = bf16[256,2048]{1,0:T(8,128)(2,1)} async-done(((bf16[1024,2048]{1,0:T(8,128)(2,1)}), bf16[256,2048]{1,0:T(8,128)(2,1)}) %reduce-scatter.9.cloned.1.call-update) | async-done | bytes 1048592 | tf_op jit(solution)/shard_map/reduce_scatter | solution.py:182
  395.3 12.5 %slice_bitcast_fusion.3 = (bf16[16,128,22,128]{3,1,2,0:T(8,128)(2,1)S(1)}, bf16[16,22,128,128]{3,2,1,0:T(8,128)(2,1)}) fusion(bf16[16,27,128,128]{3,2,1,0:T(8,128)(2,1)} %bitcast.372), kind=kLoop, calls=%fused_computation.222 | loop fusion | bytes 34603008 | tf_op jit(solution)/shard_map/tcj,rcij->tri/dot_general | solution.py:83
  407.7 5.4 copy.118
  413.1 15.1 %copy.173 = bf16[16,22,128,128]{2,3,1,0:T(8,128)(2,1)} copy(bf16[16,22,128,128]{3,2,1,0:T(8,128)(2,1)} %get-tuple-element.102) | data formatting | bytes 23068672
  438.3 18.9 %convolution_bitcast_fusion = f32[1024,2816]{1,0:T(8,128)} fusion(bf16[2816,128,16]{1,0,2:T(8,128)(2,1)} %bitcast.384, bf16[1024,2048]{1,0:T(8,128)(2,1)} %all-gather.9.cloned.1.call-done), kind=kOutput, calls=%fused_computation.49 | convolution fusion | flops 11811160064 | bytes 27262976 | tf_op jit(solution)/shard_map/tri,rcij->tcj/dot_general | solution.py:75
  457.2 15.0 %fusion.30 = (bf16[1024,1408]{1,0:T(8,128)(2,1)}, bf16[1024,1408]{1,0:T(8,128)(2,1)}, bf16[1024,1408]{1,0:T(8,128)(2,1)}) fusion(f32[1024,2816]{1,0:T(8,128)} %convolution_bitcast_fusion, bf16[1408,16,128]{2,0,1:T(8,128)(2,1)S(1)} %bitcast.389, bf16[1024,16,128]{2,1,0:T(8,128)(2,1)} %bitcast.395), kind=kOutput, calls=%fused_computation.59 | convolution fusion | flops 5928648704 | bytes 30146560 | tf_op jit(solution)/shard_map/tcj,rcij->tri/dot_general | solution.py:83
  472.2 4.5 copy.115
  476.7 4.5 copy.117
  481.3 4.5 copy.114
  485.8 4.5 copy.116
  490.3 18.1 %bitcast_convert_fusion.1 = bf16[1024,2048]{1,0:T(8,128)(2,1)} fusion(bf16[2048,22,128]{2,0,1:T(8,128)(2,1)} %bitcast.383, bf16[1024,11,128]{2,0,1:T(8,128)(2,1)} %copy.117, bf16[1024,11,128]{2,0,1:T(8,128)(2,1)} %copy.116), kind=kOutput, calls=%fused_computation.34 | convolution fusion | flops 11816140800 | bytes 21495808 | tf_op jit(solution)/shard_map/tcj,rcij->tri/dot_general | solution.py:83
  508.5 8.4 copy.110
  516.9 4.9 copy.109
  521.9 11.0 bitcast_convert_fusion.2
  533.0 6.6 convert_bitcast_fusion.1
  539.6 13.7 %reduce-scatter.13.cloned.1.call-done = bf16[256,2048]{1,0:T(8,128)(2,1)} async-done(((bf16[1024,2048]{1,0:T(8,128)(2,1)}), bf16[256,2048]{1,0:T(8,128)(2,1)}) %reduce-scatter.13.cloned.1.call-update) | async-done | bytes 1048592 | tf_op jit(solution)/shard_map/reduce_scatter | solution.py:182
  555.3 45.5 %reduce-scatter.11.cloned.1.call-done = bf16[256,2048]{1,0:T(8,128)(2,1)} async-done(((bf16[1024,2048]{1,0:T(8,128)(2,1)}), bf16[256,2048]{1,0:T(8,128)(2,1)}) %reduce-scatter.11.cloned.1.call-update) | async-done | bytes 1048592 | tf_op jit(solution)/shard_map/reduce_scatter | solution.py:182
  600.8 5.1 fusion.142
  611.2 29.3 %all-gather.13.cloned.1.call-done = bf16[1024,2048]{1,0:T(8,128)(2,1)} async-done(((bf16[256,2048]{1,0:T(8,128)(2,1)}), bf16[1024,2048]{1,0:T(8,128)(2,1)}) %all-gather.13.cloned.1.call-update) | async-done | bytes 4194320 | tf_op jit(solution)/shard_map/all_gather | solution.py:281
  640.6 5.2 bitcast_convert_fusion.5
  645.9 7.4 fusion.92
  653.3 13.0 %fusion.3 = (f32[8,512]{1,0:T(8,128)S(1)}, f32[1024,512,8]{1,0,2:T(8,128)}) fusion(f32[1,8,512,1024]{2,3,1,0:T(8,128)} %get-tuple-element.131, f32[8,512]{1,0:T(8,128)S(1)} %log_add_fusion.1, bf16[512,8,64]{0,2,1:T(8,128)(2,1)S(1)} %bitcast.394, f32[1024,640]{0,1:T(8,128)} %copy-done.15), kind=kOutput, calls=%fused_computation.9 | convolution fusion | flops 549449728 | bytes 34242560 | tf_op jit(solution)/shard_map/while/body/eval_jaxpr/qgjd,kgd->gjqk/dot_general | solution.py:158
  667.0 8.3 fusion
  675.3 7.9 fusion.18
  690.3 12.2 %fusion.17 = bf16[8,512,1024]{1,2,0:T(8,128)(2,1)S(1)} fusion(f32[1024,512,8]{1,0,2:T(8,128)} %get-tuple-element.135, f32[1,8,512,1024]{2,3,1,0:T(8,128)} %get-tuple-element.131, f32[8,512]{1,0:T(8,128)S(1)} %get-tuple-element.134, f32[8,512]{1,0:T(8,128)S(1)} %log_add_fusion.1), kind=kLoop, calls=%fused_computation.31 | loop fusion | flops 16777216 | bytes 41975808 | tf_op jit(solution)/shard_map/reshape.88
  709.3 5.0 bitcast_convert_fusion
  724.0 35.0 %reduce-scatter.15.cloned.1.call-done = bf16[256,2048]{1,0:T(8,128)(2,1)} async-done(((bf16[1024,2048]{1,0:T(8,128)(2,1)}), bf16[256,2048]{1,0:T(8,128)(2,1)}) %reduce-scatter.15.cloned.1.call-update) | async-done | bytes 1048592 | tf_op jit(solution)/shard_map/reduce_scatter | solution.py:182
  761.7 5.2 all-gather
  772.1 16.0 %convert_bitcast_fusion = bf16[16,22,128,128]{2,3,0,1:T(8,128)(2,1)S(1)} fusion(bf16[1024,11,128]{2,0,1:T(8,128)(2,1)} %copy.117, bf16[1024,11,128]{2,0,1:T(8,128)(2,1)} %copy.116, bf16[1024,2048]{1,0:T(8,128)(2,1)} %all-gather.9.cloned.1.call-done), kind=kOutput, calls=%fused_computation.23 | convolution fusion | flops 11828461568 | bytes 21495808 | tf_op jit(solution)/shard_map/tri,tcj->rcij/dot_general | solution.py:92
  788.2 11.2 convert_bitcast_fusion.4
  803.1 8.1 pad_maximum_fusion
  811.3 18.9 %copy.132 = bf16[16,27,128,128]{3,2,1,0:T(8,128)(2,1)} copy(bf16[16,27,128,128]{2,3,0,1:T(8,128)(2,1)} %pad_maximum_fusion) | data formatting | bytes 28311552 | tf_op jit(solution)/shard_map/concatenate | solution.py:317
  836.6 6.6 pad_maximum_fusion.1
  843.2 10.7 copy.138
  857.6 3.9 slice_dynamic-update-slice_fusion.4
  871.7 3.9 slice_dynamic-update-slice_fusion.2
  879.3 6.1 copy.140
  885.4 6.1 copy.141
  897.5 6.7 bitcast_convert_fusion.4
  904.2 212.1 %reduce-scatter.17.cloned.1.call-done = bf16[84,128,128]{2,1,0:T(8,128)(2,1)} async-done(((bf16[672,128,128]{2,1,0:T(8,128)(2,1)}), bf16[84,128,128]{2,1,0:T(8,128)(2,1)}) %reduce-scatter.17.cloned.1.call-update) | async-done | bytes 2752528 | tf_op jit(solution)/shard_map/reduce_scatter | solution.py:323
  1121.5 11.9 fusion.154
  1133.5 16.3 %multiply_add_fusion = (f32[84,128,128]{1,2,0:T(8,128)}, f32[84,128,128]{1,2,0:T(8,128)}) fusion(f32[84,128,128]{1,2,0:T(8,128)S(1)} %bitcast.380, f32[84,128,128]{1,2,0:T(8,128)S(1)} %bitcast.378, f32[84,128,128]{1,2,0:T(8,128)S(1)} %fusion.154, f32[84,128,128]{2,1,0:T(8,128)} %param.20), kind=kOutput, calls=%fused_computation.69 | convolution fusion | flops 2119434240 | bytes 33030144 | tf_op jit(solution)/shard_map/bij,bjk->bik/dot_general | solution.py:340
  1149.8 6.1 copy.143
  1155.9 6.2 copy.144
  1162.1 17.2 %add_multiply_fusion.1 = f32[84,128,128]{2,1,0:T(8,128)} fusion(f32[84,128,128]{2,1,0:T(8,128)} %param.18, f32[84,128,128]{2,1,0:T(8,128)} %copy-done), kind=kOutput, calls=%fused_computation.68 | convolution fusion | flops 2116681728 | bytes 16515072 | tf_op jit(solution)/shard_map/bij,bkj->bik/dot_general | solution.py:335
  1179.3 12.6 %add_multiply_fusion = f32[84,128,128]{2,1,0:T(8,128)} fusion(f32[84,128,128]{2,1,0:T(8,128)} %param.19, f32[84,128,128]{2,1,0:T(8,128)S(1)} %bitcast.360), kind=kOutput, calls=%fused_computation.67 | convolution fusion | flops 2116681728 | bytes 16515072 | tf_op jit(solution)/shard_map/bji,bjk->bik/dot_general | solution.py:336
  (253 shorter events, 127.3 us)
Async XLA Ops:
  7.2 222.6 %all-gather.7.cloned.1.call-start = ((), (), s32[]{:S(2)}) async-start(), calls=%async_computation.6 | async-start | bytes 24772608 | tf_op jit(solution)/shard_map/all_gather | solution.py:225
  11.9 373.2 %reduce-scatter.9.cloned.1.call-start = ((), (), s32[]{:S(2)}) async-start(), calls=%async_computation.7 | async-start | bytes 5242880 | tf_op jit(solution)/shard_map/reduce_scatter | solution.py:182
  26.3 8.7 copy-start.42
  35.0 6.1 copy-start.49
  35.8 245.0 %copy-start.50 = (f32[32]{0:T(128)}, f32[32]{0:T(128)S(1)}, u32[]{:S(2)}) copy-start(f32[32]{0:T(128)S(1)} %negate_power_fusion) | copy-start | bytes 388
  39.0 232.6 %copy-start.47 = (f32[1024]{0:T(1024)}, f32[1024]{0:T(1024)S(1)}, u32[]{:S(2)}) copy-start(f32[1024]{0:T(1024)S(1)} %add_rsqrt_fusion) | copy-start | bytes 12292
  39.1 241.8 %copy-start.40 = (f32[1024]{0:T(1024)}, f32[1024]{0:T(1024)S(1)}, u32[]{:S(2)}) copy-start(f32[1024]{0:T(1024)S(1)} %fusion.134) | copy-start | bytes 12292
  39.6 241.8 %copy-start.28 = (f32[1024,32]{0,1:T(8,128)}, f32[1024,32]{0,1:T(8,128)S(1)}, u32[]{:S(2)}) copy-start(f32[1024,32]{0,1:T(8,128)S(1)} %get-tuple-element.120) | copy-start | bytes 393220
  39.6 241.8 %copy-start.30 = (f32[1024,32]{0,1:T(8,128)}, f32[1024,32]{0,1:T(8,128)S(1)}, u32[]{:S(2)}) copy-start(f32[1024,32]{0,1:T(8,128)S(1)} %get-tuple-element.121) | copy-start | bytes 393220
  41.1 230.5 %copy-start.38 = (f32[1,2048]{1,0:T(1,128)}, f32[1,2048]{1,0:T(1,128)S(1)}, u32[]{:S(2)}) copy-start(f32[1,2048]{1,0:T(1,128)S(1)} %get-tuple-element.119) | copy-start | bytes 24580
  229.8 20.0 %copy-start.3 = (bf16[672,128,128]{2,1,0:T(8,128)(2,1)S(1)}, bf16[672,128,128]{2,1,0:T(8,128)(2,1)}, u32[]{:S(2)}) copy-start(bf16[672,128,128]{2,1,0:T(8,128)(2,1)} %all-gather.7.cloned.1.call-done) | copy-start | bytes 66060292
  280.6 16.6 %copy-start.15 = (f32[1024,640]{0,1:T(8,128)}, f32[1024,640]{0,1:T(8,128)S(1)}, u32[]{:S(2)}) copy-start(f32[1024,640]{0,1:T(8,128)S(1)} %fusion.76) | copy-start | bytes 7864324
  281.4 23.3 %copy-start.22 = (bf16[1024,32]{0,1:T(8,128)(2,1)}, bf16[1024,32]{0,1:T(8,128)(2,1)S(1)}, u32[]{:S(2)}) copy-start(bf16[1024,32]{0,1:T(8,128)(2,1)S(1)} %get-tuple-element.116) | copy-start | bytes 196612
  281.4 23.3 %copy-start.24 = (bf16[1024,32]{0,1:T(8,128)(2,1)}, bf16[1024,32]{0,1:T(8,128)(2,1)S(1)}, u32[]{:S(2)}) copy-start(bf16[1024,32]{0,1:T(8,128)(2,1)S(1)} %get-tuple-element.117) | copy-start | bytes 196612
  281.8 23.0 %copy-start.4 = (bf16[1,1024,1,8,32]{1,4,3,2,0:T(8,128)(2,1)}, bf16[1,1024,1,8,32]{1,4,3,2,0:T(8,128)(2,1)S(1)}, u32[]{:S(2)}) copy-start(bf16[1,1024,1,8,32]{1,4,3,2,0:T(8,128)(2,1)S(1)} %get-tuple-element.109) | copy-start | bytes 1572868
  281.8 23.0 %copy-start.6 = (bf16[1,1024,1,8,32]{1,4,3,2,0:T(8,128)(2,1)}, bf16[1,1024,1,8,32]{1,4,3,2,0:T(8,128)(2,1)S(1)}, u32[]{:S(2)}) copy-start(bf16[1,1024,1,8,32]{1,4,3,2,0:T(8,128)(2,1)S(1)} %get-tuple-element.110) | copy-start | bytes 1572868
  289.2 8.1 copy-start.34
  297.3 7.4 copy-start.43
  304.8 31.1 %copy-start.17 = (bf16[64,8,512]{2,0,1:T(8,128)(2,1)}, bf16[64,8,512]{2,0,1:T(8,128)(2,1)S(1)}, u32[]{:S(2)}) copy-start(bf16[64,8,512]{2,0,1:T(8,128)(2,1)S(1)} %fusion.86) | copy-start | bytes 1572868
  312.4 8.3 copy-start.36
  312.4 17.3 %slice-start.8 = ((s8[22020096]{0:T(1024)(128)(4,1)}), s8[1048576]{0:T(1024)(128)(4,1)S(1)}, s32[]{:S(2)}) async-start(s8[22020096]{0:T(1024)(128)(4,1)} %bitcast.375), calls=%async_computation.25 | async-start | bytes 2097152
  312.4 17.3 %slice-start.9 = ((s8[22020096]{0:T(1024)(128)(4,1)}), s8[4194304]{0:T(1024)(128)(4,1)S(1)}, s32[]{:S(2)}) async-start(s8[22020096]{0:T(1024)(128)(4,1)} %bitcast.375), calls=%async_computation.26 | async-start | bytes 8388608
  320.6 9.0 copy-start.45
  320.6 9.0 slice-start.10
  320.6 9.0 slice-start.11
  320.7 9.5 slice-start.12
  320.7 10.7 slice-start.13
  331.4 9.1 copy-start.19
  340.5 48.3 %copy-start.52 = (s32[1,1024]{1,0:T(1,128)S(1)}, s32[1,1024]{1,0:T(1,128)}, u32[]{:S(2)}) copy-start(s32[1,1024]{1,0:T(1,128)} %param.13) | copy-start | bytes 12292
  340.5 97.8 %all-gather.9.cloned.1.call-start = ((), (), s32[]{:S(2)}) async-start(), calls=%async_computation.8 | async-start | bytes 5242880 | tf_op jit(solution)/shard_map/all_gather | solution.py:257
  388.7 164.6 %reduce-scatter.13.cloned.1.call-start = ((), (), s32[]{:S(2)}) async-start(), calls=%async_computation.11 | async-start | bytes 5242880 | tf_op jit(solution)/shard_map/reduce_scatter | solution.py:182
  438.3 18.9 %copy-start.11 = (bf16[11,16,128,128]{3,2,0,1:T(8,128)(2,1)S(1)}, bf16[11,16,128,128]{3,2,0,1:T(8,128)(2,1)}, u32[]{:S(2)}) copy-start(bf16[11,16,128,128]{3,2,0,1:T(8,128)(2,1)} %copy.112) | copy-start | bytes 17301508
  508.5 92.3 %reduce-scatter.11.cloned.1.call-start = ((), (), s32[]{:S(2)}) async-start(), calls=%async_computation.9 | async-start | bytes 5242880 | tf_op jit(solution)/shard_map/reduce_scatter | solution.py:182
  532.8 107.7 %all-gather.13.cloned.1.call-start = ((), (), s32[]{:S(2)}) async-start(), calls=%async_computation.12 | async-start | bytes 5242880 | tf_op jit(solution)/shard_map/all_gather | solution.py:281
  605.9 5.3 copy-start.37
  605.9 5.3 copy-start.46
  605.9 5.3 copy-start.35
  605.9 5.3 copy-start.44
  605.9 153.0 %reduce-scatter.15.cloned.1.call-start = ((), (), s32[]{:S(2)}) async-start(), calls=%async_computation.13 | async-start | bytes 5242880 | tf_op jit(solution)/shard_map/reduce_scatter | solution.py:182
  645.9 20.4 %slice-start = ((s8[16777216]{0:T(1024)(128)(4,1)}), s8[4194304]{0:T(1024)(128)(4,1)S(1)}, s32[]{:S(2)}) async-start(s8[16777216]{0:T(1024)(128)(4,1)} %bitcast.357), calls=%async_computation.17 | async-start | bytes 8388608
  645.9 20.4 %slice-start.1 = ((s8[16777216]{0:T(1024)(128)(4,1)}), s8[4194304]{0:T(1024)(128)(4,1)S(1)}, s32[]{:S(2)}) async-start(s8[16777216]{0:T(1024)(128)(4,1)} %bitcast.357), calls=%async_computation.18 | async-start | bytes 8388608
  653.3 13.0 %slice-start.2 = ((s8[16777216]{0:T(1024)(128)(4,1)}), s8[4194304]{0:T(1024)(128)(4,1)S(1)}, s32[]{:S(2)}) async-start(s8[16777216]{0:T(1024)(128)(4,1)} %bitcast.357), calls=%async_computation.19 | async-start | bytes 8388608
  653.3 13.7 %slice-start.3 = ((s8[16777216]{0:T(1024)(128)(4,1)}), s8[4194304]{0:T(1024)(128)(4,1)S(1)}, s32[]{:S(2)}) async-start(s8[16777216]{0:T(1024)(128)(4,1)} %bitcast.357), calls=%async_computation.20 | async-start | bytes 8388608
  675.3 7.9 copy-start.5
  675.3 7.9 copy-start.7
  709.3 5.9 copy-start.48
  709.3 5.9 copy-start.39
  714.3 177.2 %all-gather.11.cloned.1.call-start = ((), (), s32[]{:S(2)}) async-start(), calls=%async_computation.10 | async-start | bytes 5242880 | tf_op jit(solution)/shard_map/all_gather | solution.py:264
  715.1 176.4 %reduce-scatter.19.cloned.1.call-start = ((), (), s32[]{:S(2)}) async-start(), calls=%async_computation.16 | async-start | bytes 1179648
  722.0 46.5 %copy-start.10 = (f32[256,2048]{1,0:T(8,128)S(1)}, f32[256,2048]{1,0:T(8,128)}, u32[]{:S(2)}) copy-start(f32[256,2048]{1,0:T(8,128)} %get-tuple-element.92) | copy-start | bytes 6291460
  759.0 9.5 copy-start.14
  768.4 129.1 %all-gather.15.cloned.1.call-start = ((), (), s32[]{:S(2)}) async-start(), calls=%async_computation.14 | async-start | bytes 5242880 | tf_op jit(solution)/shard_map/all_gather | solution.py:311
  772.1 344.2 %reduce-scatter.17.cloned.1.call-start = ((), (), s32[]{:S(2)}) async-start(), calls=%async_computation.15 | async-start | bytes 24772608 | tf_op jit(solution)/shard_map/reduce_scatter | solution.py:323
  788.2 11.2 copy-start.13
  788.2 11.2 copy-start.27
  853.8 11.4 slice-start.6
  857.6 7.6 slice-start.7
  1116.3 17.2 %slice-start.15 = ((s8[5505024]{0:T(1024)(128)(4,1)}), s8[4194304]{0:T(1024)(128)(4,1)S(1)}, s32[]{:S(2)}) async-start(s8[5505024]{0:T(1024)(128)(4,1)} %bitcast.377), calls=%async_computation.32 | async-start | bytes 8388608
  1116.3 17.2 %slice-start.17 = ((s8[5505024]{0:T(1024)(128)(4,1)}), s8[4194304]{0:T(1024)(128)(4,1)S(1)}, s32[]{:S(2)}) async-start(s8[5505024]{0:T(1024)(128)(4,1)} %bitcast.379), calls=%async_computation.34 | async-start | bytes 8388608
  1121.5 12.0 slice-start.16
  1121.5 12.0 slice-start.18
  1155.9 23.3 %slice-start.4 = ((s8[5505024]{0:T(1024)(128)(4,1)}), s8[1310720]{0:T(1024)(128)(4,1)S(1)}, s32[]{:S(2)}) async-start(s8[5505024]{0:T(1024)(128)(4,1)} %bitcast.359), calls=%async_computation.21 | async-start | bytes 2621440
  1162.1 17.2 %slice-start.5 = ((s8[5505024]{0:T(1024)(128)(4,1)}), s8[4194304]{0:T(1024)(128)(4,1)S(1)}, s32[]{:S(2)}) async-start(s8[5505024]{0:T(1024)(128)(4,1)} %bitcast.359), calls=%async_computation.22 | async-start | bytes 8388608
  1179.2 12.6 %copy-start.12 = (bf16[1024,2048]{1,0:T(8,128)(2,1)S(1)}, bf16[1024,2048]{1,0:T(8,128)(2,1)}, u32[]{:S(2)}) copy-start(bf16[1024,2048]{1,0:T(8,128)(2,1)} %all-gather.11.cloned.1.call-done) | copy-start | bytes 12582916
  (19 other events, 56.8 us)
Sparse Core Ops, SparseCore 0:
  12.0 217.6 all-gather.6
  340.6 44.5 reduce-scatter.8
  388.8 34.4 all-gather.8
  508.6 44.6 reduce-scatter.12
  556.3 44.4 reduce-scatter.10
  606.1 34.4 all-gather.12
  714.4 44.4 reduce-scatter.14
  760.5 34.4 all-gather.10
  798.4 63.4 reduce-scatter.18
  864.0 33.4 all-gather.14
  900.0 216.2 reduce-scatter.16
where the time goes:
time: 1210 us; the launch traced here: 1200 us
  waiting for transfers between devices  574 us (47%)
  matrix products  249 us (21%)
  local copies, waits for them, and re-layouts  235 us (19%)
  other arithmetic  122 us (10%)
  between operations  15.1 us (1%)
    reduce_scatter x1, waiting for transfers between devices, on_device(): lax.psum_scatter(jnp.concatenate([all_grads[rank * own:(rank + 1) * own]...  212 us
    all_gather x1, waiting for transfers between devices, on_device(): lax.all_gather(weights_low, 'dp', axis=0, tiled=True, axis_index_groups=[...  189 us
    reduce_scatter x4, waiting for transfers between devices, sum_rows(): lax.psum_scatter(values.astype(jnp.bfloat16), 'mp', scatter_dimension=0,...  139 us
    unnamed x165, local copies, waits for them, and re-layouts  119 us
    dot_general x4, matrix products, project_back(): jnp.einsum('tcj,rcij->tri', shaped, weights, preferred_element_type=jnp.f...  43.4 us
    dot_general x4, matrix products, project(): jnp.einsum('tri,rcij->tcj', shaped, weights, preferred_element_type=jnp.f...  43.3 us
    dot_general x4, matrix products, weight_grad(): jnp.einsum('tri,tcj->rcij', left_shaped, right_shaped, preferred_element_...  33.7 us
    all_gather x1, waiting for transfers between devices, on_device(): lax.all_gather(middle_grad.astype(jnp.bfloat16), 'mp', axis=0, tiled=True)  29.3 us
  transfers between devices with their start and end apart: 11, of which 8 were waited for; matrix products, arithmetic and copies ran while one was open for 21% of the time, Pallas kernels for 0%

commit v1 on v0

--- a/solution.py
+++ b/solution.py
@@ -278,7 +278,12 @@
         second_grad, second_unit, second_scale, norm_gains[1]
     )
     second_gain = jnp.sum(second_grad * second_unit, axis=0)
-    attn_grad = lax.all_gather(middle_grad.astype(jnp.bfloat16), "mp", axis=0, tiled=True)
+    attn_grad = jnp.concatenate(
+        lax.all_to_all(
+            jnp.stack([middle_grad.astype(jnp.bfloat16)] * lax.axis_size("mp")), "mp", 0, 0
+        ),
+        axis=0,
+    )
     grad_attn_out = weight_grad(mixed_use, attn_grad, block_size)
     mixed_grad = (
         project_back(attn_grad, w_attn_out)

time: 1210 us -> 1230 us (1.017)
  waiting for transfers between devices: 574 us -> 588 us
    all_to_all x0 -> x1, waiting for transfers between devices: none -> 43.6 us  [on_device(): lax.all_to_all(jnp.stack([middle_grad.astype(jnp.bfloat16)] * lax.axis_si...]
    all_gather x1 -> x0, waiting for transfers between devices: 29.3 us -> none  [on_device(): lax.all_gather(middle_grad.astype(jnp.bfloat16), 'mp', axis=0, tiled=True)]
    unnamed x165 -> x171, local copies, waits for them, and re-layouts: 119 us -> 121 us
where the time goes in v1:
time: 1230 us; the launch traced here: 1220 us
  waiting for transfers between devices  588 us (48%)
  matrix products  249 us (20%)
  local copies, waits for them, and re-layouts  237 us (19%)
  other arithmetic  122 us (10%)
  between operations  15.5 us (1%)
    reduce_scatter x1, waiting for transfers between devices, on_device(): lax.psum_scatter(jnp.concatenate([all_grads[rank * own:(rank + 1) * own]...  212 us
    all_gather x1, waiting for transfers between devices, on_device(): lax.all_gather(weights_low, 'dp', axis=0, tiled=True, axis_index_groups=[...  189 us
    reduce_scatter x4, waiting for transfers between devices, sum_rows(): lax.psum_scatter(values.astype(jnp.bfloat16), 'mp', scatter_dimension=0,...  139 us
    unnamed x171, local copies, waits for them, and re-layouts  121 us
    all_to_all x1, waiting for transfers between devices, on_device(): lax.all_to_all(jnp.stack([middle_grad.astype(jnp.bfloat16)] * lax.axis_si...  43.6 us
    dot_general x4, matrix products, project(): jnp.einsum('tri,rcij->tcj', shaped, weights, preferred_element_type=jnp.f...  43.3 us
    dot_general x4, matrix products, project_back(): jnp.einsum('tcj,rcij->tri', shaped, weights, preferred_element_type=jnp.f...  40.5 us
    dot_general x4, matrix products, weight_grad(): jnp.einsum('tri,tcj->rcij', left_shaped, right_shaped, preferred_element_...  35.9 us
  transfers between devices with their start and end apart: 11, of which 8 were waited for; matrix products, arithmetic and copies ran while one was open for 21% of the time, Pallas kernels for 0%

profile of v1, /device:TPU:0, one launch (start us, length us, event | category | flops | bytes accessed | tf_op | source)
XLA Modules:
  0.0 1221.6 jit_solution(11990858947721560008)
XLA Ops:
  7.2 4.7 convert_element_type.160
  12.0 14.3 %convert_bitcast_fusion.2 = (f32[1024,2048]{1,0:T(8,128)}, f32[128,8,16,128]{3,1,2,0:T(8,128)}, f32[1,1024,2048]{2,1,0:T(8,128)}) fusion(bf16[1,1024,2048]{2,1,0:T(8,128)(2,1)} %param.11), kind=kLoop, calls=%fused_computation.50 | loop fusion | flops 2097152 | bytes 29360128 | tf_op jit(solution)/shard_map/reshape | solution.py:238
  26.3 8.7 copy.176
  41.1 188.6 %all-gather.6.cloned.1.call-done = bf16[672,128,128]{2,1,0:T(8,128)(2,1)} async-done(((bf16[84,128,128]{2,1,0:T(8,128)(2,1)}), bf16[672,128,128]{2,1,0:T(8,128)(2,1)}) %all-gather.6.cloned.1.call-update) | async-done | bytes 22020112 | tf_op jit(solution)/shard_map/all_gather | solution.py:225
  233.6 4.4 slice_dynamic-update-slice_fusion.9
  238.0 4.5 slice_dynamic-update-slice_fusion.8
  253.6 7.7 slice.234
  261.3 5.0 copy-done.1
  271.6 9.0 fusion.75
  282.1 7.2 fusion.147
  289.2 8.0 fusion.7
  297.3 7.4 fusion.85
  304.8 7.6 fusion.148
  312.4 8.2 fusion.6
  320.7 9.0 fusion.82
  336.0 4.4 bitcast_convert_fusion.3
  340.5 44.6 %reduce-scatter.9.cloned.1.call-done = bf16[256,2048]{1,0:T(8,128)(2,1)} async-done(((bf16[1024,2048]{1,0:T(8,128)(2,1)}), bf16[256,2048]{1,0:T(8,128)(2,1)}) %reduce-scatter.9.cloned.1.call-update) | async-done | bytes 1048592 | tf_op jit(solution)/shard_map/reduce_scatter | solution.py:182
  395.2 12.5 %slice_bitcast_fusion.3 = (bf16[16,128,22,128]{3,1,2,0:T(8,128)(2,1)S(1)}, bf16[16,22,128,128]{3,2,1,0:T(8,128)(2,1)}) fusion(bf16[16,27,128,128]{3,2,1,0:T(8,128)(2,1)} %bitcast.364), kind=kLoop, calls=%fused_computation.221 | loop fusion | bytes 34603008 | tf_op jit(solution)/shard_map/tcj,rcij->tri/dot_general | solution.py:83
  407.7 5.4 copy.117
  413.1 15.1 %copy.172 = bf16[16,22,128,128]{2,3,1,0:T(8,128)(2,1)} copy(bf16[16,22,128,128]{3,2,1,0:T(8,128)(2,1)} %get-tuple-element.102) | data formatting | bytes 23068672
  438.3 18.9 %convolution_bitcast_fusion = f32[1024,2816]{1,0:T(8,128)} fusion(bf16[2816,128,16]{1,0,2:T(8,128)(2,1)} %bitcast.376, bf16[1024,2048]{1,0:T(8,128)(2,1)} %all-gather.8.cloned.1.call-done), kind=kOutput, calls=%fused_computation.49 | convolution fusion | flops 11811160064 | bytes 27262976 | tf_op jit(solution)/shard_map/tri,rcij->tcj/dot_general | solution.py:75
  457.2 15.0 %fusion.30 = (bf16[1024,1408]{1,0:T(8,128)(2,1)}, bf16[1024,1408]{1,0:T(8,128)(2,1)}, bf16[1024,1408]{1,0:T(8,128)(2,1)}) fusion(f32[1024,2816]{1,0:T(8,128)} %convolution_bitcast_fusion, bf16[1408,16,128]{2,0,1:T(8,128)(2,1)S(1)} %bitcast.381, bf16[1024,16,128]{2,1,0:T(8,128)(2,1)} %bitcast.387), kind=kOutput, calls=%fused_computation.59 | convolution fusion | flops 5928648704 | bytes 30146560 | tf_op jit(solution)/shard_map/tcj,rcij->tri/dot_general | solution.py:83
  472.2 4.5 copy.114
  476.8 4.5 copy.116
  481.3 4.5 copy.113
  485.8 4.5 copy.115
  490.4 18.1 %bitcast_convert_fusion.1 = bf16[1024,2048]{1,0:T(8,128)(2,1)} fusion(bf16[2048,22,128]{2,0,1:T(8,128)(2,1)} %bitcast.375, bf16[1024,11,128]{2,0,1:T(8,128)(2,1)} %copy.116, bf16[1024,11,128]{2,0,1:T(8,128)(2,1)} %copy.115), kind=kOutput, calls=%fused_computation.34 | convolution fusion | flops 11816140800 | bytes 21495808 | tf_op jit(solution)/shard_map/tcj,rcij->tri/dot_general | solution.py:83
  508.6 8.4 copy.109
  516.9 4.9 copy.108
  521.8 11.0 bitcast_convert_fusion.2
  532.9 6.6 convert_bitcast_fusion.1
  539.5 13.8 %reduce-scatter.13.cloned.1.call-done = bf16[256,2048]{1,0:T(8,128)(2,1)} async-done(((bf16[1024,2048]{1,0:T(8,128)(2,1)}), bf16[256,2048]{1,0:T(8,128)(2,1)}) %reduce-scatter.13.cloned.1.call-update) | async-done | bytes 1048592 | tf_op jit(solution)/shard_map/reduce_scatter | solution.py:182
  555.3 45.5 %reduce-scatter.11.cloned.1.call-done = bf16[256,2048]{1,0:T(8,128)(2,1)} async-done(((bf16[1024,2048]{1,0:T(8,128)(2,1)}), bf16[256,2048]{1,0:T(8,128)(2,1)}) %reduce-scatter.11.cloned.1.call-update) | async-done | bytes 1048592 | tf_op jit(solution)/shard_map/reduce_scatter | solution.py:182
  600.8 4.7 fusion.141
  608.0 4.9 all-to-all-start
  617.6 43.6 %all-to-all-done = bf16[4,256,2048]{2,1,0:T(8,128)(2,1)} async-done(((bf16[4,256,2048]{2,1,0:T(8,128)(2,1)}), bf16[4,256,2048]{2,1,0:T(8,128)(2,1)}, u32[]{:S(2)}, u32[]{:S(2)}) %all-to-all-start) | async-done | bytes 4194336 | tf_op jit(solution)/shard_map/all_to_all | solution.py:282
  667.3 7.4 fusion.91
  674.6 13.0 %fusion.3 = (f32[8,512]{1,0:T(8,128)S(1)}, f32[1024,512,8]{1,0,2:T(8,128)}) fusion(f32[1,8,512,1024]{2,3,1,0:T(8,128)} %get-tuple-element.131, f32[8,512]{1,0:T(8,128)S(1)} %log_add_fusion.1, bf16[512,8,64]{0,2,1:T(8,128)(2,1)S(1)} %bitcast.386, f32[1024,640]{0,1:T(8,128)} %copy-done.17), kind=kOutput, calls=%fused_computation.9 | convolution fusion | flops 549449728 | bytes 34242560 | tf_op jit(solution)/shard_map/while/body/eval_jaxpr/qgjd,kgd->gjqk/dot_general | solution.py:158
  688.4 8.3 fusion
  696.6 7.9 fusion.18
  711.6 12.2 %fusion.17 = bf16[8,512,1024]{1,2,0:T(8,128)(2,1)S(1)} fusion(f32[1024,512,8]{1,0,2:T(8,128)} %get-tuple-element.135, f32[1,8,512,1024]{2,3,1,0:T(8,128)} %get-tuple-element.131, f32[8,512]{1,0:T(8,128)S(1)} %get-tuple-element.134, f32[8,512]{1,0:T(8,128)S(1)} %log_add_fusion.1), kind=kLoop, calls=%fused_computation.31 | loop fusion | flops 16777216 | bytes 41975808 | tf_op jit(solution)/shard_map/reshape.87
  730.6 5.0 bitcast_convert_fusion
  745.3 35.0 %reduce-scatter.15.cloned.1.call-done = bf16[256,2048]{1,0:T(8,128)(2,1)} async-done(((bf16[1024,2048]{1,0:T(8,128)(2,1)}), bf16[256,2048]{1,0:T(8,128)(2,1)}) %reduce-scatter.15.cloned.1.call-update) | async-done | bytes 1048592 | tf_op jit(solution)/shard_map/reduce_scatter | solution.py:182
  783.0 5.2 all-gather
  793.5 16.0 %convert_bitcast_fusion = bf16[16,22,128,128]{2,3,0,1:T(8,128)(2,1)S(1)} fusion(bf16[1024,11,128]{2,0,1:T(8,128)(2,1)} %copy.116, bf16[1024,11,128]{2,0,1:T(8,128)(2,1)} %copy.115, bf16[1024,2048]{1,0:T(8,128)(2,1)} %all-gather.8.cloned.1.call-done), kind=kOutput, calls=%fused_computation.23 | convolution fusion | flops 11828461568 | bytes 21495808 | tf_op jit(solution)/shard_map/tri,tcj->rcij/dot_general | solution.py:92
  809.5 11.2 convert_bitcast_fusion.4
  824.5 8.2 pad_maximum_fusion
  832.6 19.1 %copy.131 = bf16[16,27,128,128]{3,2,1,0:T(8,128)(2,1)} copy(bf16[16,27,128,128]{2,3,0,1:T(8,128)(2,1)} %pad_maximum_fusion) | data formatting | bytes 28311552 | tf_op jit(solution)/shard_map/concatenate | solution.py:322
  851.7 4.9 convert_bitcast_fusion.6
  856.6 6.6 pad_maximum_fusion.1
  863.2 10.7 copy.137
  877.7 3.9 slice_dynamic-update-slice_fusion.4
  891.8 4.2 slice_dynamic-update-slice_fusion.2
  899.7 6.1 copy.139
  905.8 6.1 copy.140
  914.2 4.2 all-gather.12.cloned.1.call-done
  918.4 6.7 bitcast_convert_fusion.4
  925.1 211.9 %reduce-scatter.17.cloned.1.call-done = bf16[84,128,128]{2,1,0:T(8,128)(2,1)} async-done(((bf16[672,128,128]{2,1,0:T(8,128)(2,1)}), bf16[84,128,128]{2,1,0:T(8,128)(2,1)}) %reduce-scatter.17.cloned.1.call-update) | async-done | bytes 2752528 | tf_op jit(solution)/shard_map/reduce_scatter | solution.py:328
  1142.3 11.9 fusion.153
  1154.3 16.3 %multiply_add_fusion = (f32[84,128,128]{1,2,0:T(8,128)}, f32[84,128,128]{1,2,0:T(8,128)}) fusion(f32[84,128,128]{1,2,0:T(8,128)S(1)} %bitcast.372, f32[84,128,128]{1,2,0:T(8,128)S(1)} %bitcast.370, f32[84,128,128]{1,2,0:T(8,128)S(1)} %fusion.153, f32[84,128,128]{2,1,0:T(8,128)} %param.20), kind=kOutput, calls=%fused_computation.69 | convolution fusion | flops 2119434240 | bytes 33030144 | tf_op jit(solution)/shard_map/bij,bjk->bik/dot_general | solution.py:345
  1170.6 6.1 copy.142
  1176.7 6.2 copy.143
  1182.8 17.2 %add_multiply_fusion.1 = f32[84,128,128]{2,1,0:T(8,128)} fusion(f32[84,128,128]{2,1,0:T(8,128)} %param.18, f32[84,128,128]{2,1,0:T(8,128)} %copy-done), kind=kOutput, calls=%fused_computation.68 | convolution fusion | flops 2116681728 | bytes 16515072 | tf_op jit(solution)/shard_map/bij,bkj->bik/dot_general | solution.py:340
  1200.0 12.6 %add_multiply_fusion = f32[84,128,128]{2,1,0:T(8,128)} fusion(f32[84,128,128]{2,1,0:T(8,128)} %param.19, f32[84,128,128]{2,1,0:T(8,128)S(1)} %bitcast.352), kind=kOutput, calls=%fused_computation.67 | convolution fusion | flops 2116681728 | bytes 16515072 | tf_op jit(solution)/shard_map/bji,bjk->bik/dot_general | solution.py:341
  (259 shorter events, 132.6 us)
Async XLA Ops:
  7.2 222.6 %all-gather.6.cloned.1.call-start = ((), (), s32[]{:S(2)}) async-start(), calls=%async_computation.7 | async-start | bytes 24772608 | tf_op jit(solution)/shard_map/all_gather | solution.py:225
  11.9 373.2 %reduce-scatter.9.cloned.1.call-start = ((), (), s32[]{:S(2)}) async-start(), calls=%async_computation.8 | async-start | bytes 5242880 | tf_op jit(solution)/shard_map/reduce_scatter | solution.py:182
  26.3 8.7 copy-start.45
  35.0 6.1 copy-start.52
  35.8 245.0 %copy-start.53 = (f32[32]{0:T(128)}, f32[32]{0:T(128)S(1)}, u32[]{:S(2)}) copy-start(f32[32]{0:T(128)S(1)} %negate_power_fusion) | copy-start | bytes 388
  39.0 232.6 %copy-start.50 = (f32[1024]{0:T(1024)}, f32[1024]{0:T(1024)S(1)}, u32[]{:S(2)}) copy-start(f32[1024]{0:T(1024)S(1)} %add_rsqrt_fusion) | copy-start | bytes 12292
  39.1 241.8 %copy-start.43 = (f32[1024]{0:T(1024)}, f32[1024]{0:T(1024)S(1)}, u32[]{:S(2)}) copy-start(f32[1024]{0:T(1024)S(1)} %fusion.133) | copy-start | bytes 12292
  39.6 241.8 %copy-start.31 = (f32[1024,32]{0,1:T(8,128)}, f32[1024,32]{0,1:T(8,128)S(1)}, u32[]{:S(2)}) copy-start(f32[1024,32]{0,1:T(8,128)S(1)} %get-tuple-element.120) | copy-start | bytes 393220
  39.6 241.8 %copy-start.33 = (f32[1024,32]{0,1:T(8,128)}, f32[1024,32]{0,1:T(8,128)S(1)}, u32[]{:S(2)}) copy-start(f32[1024,32]{0,1:T(8,128)S(1)} %get-tuple-element.121) | copy-start | bytes 393220
  41.1 230.5 %copy-start.41 = (f32[1,2048]{1,0:T(1,128)}, f32[1,2048]{1,0:T(1,128)S(1)}, u32[]{:S(2)}) copy-start(f32[1,2048]{1,0:T(1,128)S(1)} %get-tuple-element.119) | copy-start | bytes 24580
  229.8 20.0 %copy-start.3 = (bf16[672,128,128]{2,1,0:T(8,128)(2,1)S(1)}, bf16[672,128,128]{2,1,0:T(8,128)(2,1)}, u32[]{:S(2)}) copy-start(bf16[672,128,128]{2,1,0:T(8,128)(2,1)} %all-gather.6.cloned.1.call-done) | copy-start | bytes 66060292
  280.6 16.6 %copy-start.17 = (f32[1024,640]{0,1:T(8,128)}, f32[1024,640]{0,1:T(8,128)S(1)}, u32[]{:S(2)}) copy-start(f32[1024,640]{0,1:T(8,128)S(1)} %fusion.75) | copy-start | bytes 7864324
  281.4 23.3 %copy-start.25 = (bf16[1024,32]{0,1:T(8,128)(2,1)}, bf16[1024,32]{0,1:T(8,128)(2,1)S(1)}, u32[]{:S(2)}) copy-start(bf16[1024,32]{0,1:T(8,128)(2,1)S(1)} %get-tuple-element.116) | copy-start | bytes 196612
  281.4 23.3 %copy-start.27 = (bf16[1024,32]{0,1:T(8,128)(2,1)}, bf16[1024,32]{0,1:T(8,128)(2,1)S(1)}, u32[]{:S(2)}) copy-start(bf16[1024,32]{0,1:T(8,128)(2,1)S(1)} %get-tuple-element.117) | copy-start | bytes 196612
  281.8 23.0 %copy-start.5 = (bf16[1,1024,1,8,32]{1,4,3,2,0:T(8,128)(2,1)}, bf16[1,1024,1,8,32]{1,4,3,2,0:T(8,128)(2,1)S(1)}, u32[]{:S(2)}) copy-start(bf16[1,1024,1,8,32]{1,4,3,2,0:T(8,128)(2,1)S(1)} %get-tuple-element.109) | copy-start | bytes 1572868
  281.8 23.0 %copy-start.7 = (bf16[1,1024,1,8,32]{1,4,3,2,0:T(8,128)(2,1)}, bf16[1,1024,1,8,32]{1,4,3,2,0:T(8,128)(2,1)S(1)}, u32[]{:S(2)}) copy-start(bf16[1,1024,1,8,32]{1,4,3,2,0:T(8,128)(2,1)S(1)} %get-tuple-element.110) | copy-start | bytes 1572868
  289.2 8.1 copy-start.37
  297.3 7.4 copy-start.46
  304.8 31.1 %copy-start.20 = (bf16[64,8,512]{2,0,1:T(8,128)(2,1)}, bf16[64,8,512]{2,0,1:T(8,128)(2,1)S(1)}, u32[]{:S(2)}) copy-start(bf16[64,8,512]{2,0,1:T(8,128)(2,1)S(1)} %fusion.85) | copy-start | bytes 1572868
  312.4 8.3 copy-start.39
  312.4 17.3 %slice-start.8 = ((s8[22020096]{0:T(1024)(128)(4,1)}), s8[1048576]{0:T(1024)(128)(4,1)S(1)}, s32[]{:S(2)}) async-start(s8[22020096]{0:T(1024)(128)(4,1)} %bitcast.367), calls=%async_computation.25 | async-start | bytes 2097152
  312.4 17.3 %slice-start.9 = ((s8[22020096]{0:T(1024)(128)(4,1)}), s8[4194304]{0:T(1024)(128)(4,1)S(1)}, s32[]{:S(2)}) async-start(s8[22020096]{0:T(1024)(128)(4,1)} %bitcast.367), calls=%async_computation.26 | async-start | bytes 8388608
  320.6 9.0 copy-start.48
  320.6 9.0 slice-start.10
  320.6 9.0 slice-start.11
  320.7 9.5 slice-start.12
  320.7 10.7 slice-start.13
  331.3 9.1 copy-start.22
  340.5 48.2 %copy-start.55 = (s32[1,1024]{1,0:T(1,128)S(1)}, s32[1,1024]{1,0:T(1,128)}, u32[]{:S(2)}) copy-start(s32[1,1024]{1,0:T(1,128)} %param.13) | copy-start | bytes 12292
  340.5 97.8 %all-gather.8.cloned.1.call-start = ((), (), s32[]{:S(2)}) async-start(), calls=%async_computation.9 | async-start | bytes 5242880 | tf_op jit(solution)/shard_map/all_gather | solution.py:257
  388.6 164.6 %reduce-scatter.13.cloned.1.call-start = ((), (), s32[]{:S(2)}) async-start(), calls=%async_computation.12 | async-start | bytes 5242880 | tf_op jit(solution)/shard_map/reduce_scatter | solution.py:182
  438.3 18.9 %copy-start.12 = (bf16[11,16,128,128]{3,2,0,1:T(8,128)(2,1)S(1)}, bf16[11,16,128,128]{3,2,0,1:T(8,128)(2,1)}, u32[]{:S(2)}) copy-start(bf16[11,16,128,128]{3,2,0,1:T(8,128)(2,1)} %copy.111) | copy-start | bytes 17301508
  508.5 92.2 %reduce-scatter.11.cloned.1.call-start = ((), (), s32[]{:S(2)}) async-start(), calls=%async_computation.10 | async-start | bytes 5242880 | tf_op jit(solution)/shard_map/reduce_scatter | solution.py:182
  605.5 7.7 copy-start.4
  608.0 53.1 %all-to-all-start = ((bf16[4,256,2048]{2,1,0:T(8,128)(2,1)}), bf16[4,256,2048]{2,1,0:T(8,128)(2,1)}, u32[]{:S(2)}, u32[]{:S(2)}) async-start(bf16[4,256,2048]{2,1,0:T(8,128)(2,1)} %stack.16), calls=%async_computation.3 | async-start | bytes 8388608 | tf_op jit(solution)/shard_map/all_to_all | solution.py:282
  613.0 167.3 %reduce-scatter.15.cloned.1.call-start = ((), (), s32[]{:S(2)}) async-start(), calls=%async_computation.13 | async-start | bytes 5242880 | tf_op jit(solution)/shard_map/reduce_scatter | solution.py:182
  617.5 47.2 %copy-start.19 = (bf16[4,16,128,128]{3,2,0,1:T(8,128)(2,1)S(1)}, bf16[4,16,128,128]{3,2,0,1:T(8,128)(2,1)}, u32[]{:S(2)}) copy-start(bf16[4,16,128,128]{3,2,0,1:T(8,128)(2,1)} %copy.118) | copy-start | bytes 6291460
  667.2 20.4 %slice-start = ((s8[16777216]{0:T(1024)(128)(4,1)}), s8[4194304]{0:T(1024)(128)(4,1)S(1)}, s32[]{:S(2)}) async-start(s8[16777216]{0:T(1024)(128)(4,1)} %bitcast.349), calls=%async_computation.17 | async-start | bytes 8388608
  667.2 20.4 %slice-start.1 = ((s8[16777216]{0:T(1024)(128)(4,1)}), s8[4194304]{0:T(1024)(128)(4,1)S(1)}, s32[]{:S(2)}) async-start(s8[16777216]{0:T(1024)(128)(4,1)} %bitcast.349), calls=%async_computation.18 | async-start | bytes 8388608
  674.6 13.0 %slice-start.2 = ((s8[16777216]{0:T(1024)(128)(4,1)}), s8[4194304]{0:T(1024)(128)(4,1)S(1)}, s32[]{:S(2)}) async-start(s8[16777216]{0:T(1024)(128)(4,1)} %bitcast.349), calls=%async_computation.19 | async-start | bytes 8388608
  674.6 13.7 %slice-start.3 = ((s8[16777216]{0:T(1024)(128)(4,1)}), s8[4194304]{0:T(1024)(128)(4,1)S(1)}, s32[]{:S(2)}) async-start(s8[16777216]{0:T(1024)(128)(4,1)} %bitcast.349), calls=%async_computation.20 | async-start | bytes 8388608
  696.6 7.9 copy-start.6
  696.6 7.9 copy-start.8
  730.6 5.8 copy-start.51
  730.6 5.9 copy-start.42
  735.6 176.3 %all-gather.10.cloned.1.call-start = ((), (), s32[]{:S(2)}) async-start(), calls=%async_computation.11 | async-start | bytes 5242880 | tf_op jit(solution)/shard_map/all_gather | solution.py:264
  736.4 175.6 %reduce-scatter.19.cloned.1.call-start = ((), (), s32[]{:S(2)}) async-start(), calls=%async_computation.16 | async-start | bytes 1179648
  743.3 46.5 %copy-start.11 = (f32[256,2048]{1,0:T(8,128)S(1)}, f32[256,2048]{1,0:T(8,128)}, u32[]{:S(2)}) copy-start(f32[256,2048]{1,0:T(8,128)} %get-tuple-element.92) | copy-start | bytes 6291460
  780.3 9.5 copy-start.16
  789.7 128.7 %all-gather.12.cloned.1.call-start = ((), (), s32[]{:S(2)}) async-start(), calls=%async_computation.14 | async-start | bytes 5242880 | tf_op jit(solution)/shard_map/all_gather | solution.py:316
  793.4 343.6 %reduce-scatter.17.cloned.1.call-start = ((), (), s32[]{:S(2)}) async-start(), calls=%async_computation.15 | async-start | bytes 24772608 | tf_op jit(solution)/shard_map/reduce_scatter | solution.py:328
  809.5 11.2 copy-start.15
  809.5 11.2 copy-start.30
  832.6 19.1 %copy-start.35 = (bf16[512,4,128]{2,0,1:T(8,128)(2,1)S(1)}, bf16[512,4,128]{2,0,1:T(8,128)(2,1)}, u32[]{:S(2)}) copy-start(bf16[512,4,128]{2,0,1:T(8,128)(2,1)} %copy.133) | copy-start | bytes 1572868
  832.6 19.1 %copy-start.36 = (bf16[512,4,128]{2,0,1:T(8,128)(2,1)S(1)}, bf16[512,4,128]{2,0,1:T(8,128)(2,1)}, u32[]{:S(2)}) copy-start(bf16[512,4,128]{2,0,1:T(8,128)(2,1)} %copy.132) | copy-start | bytes 1572868
  873.9 11.4 slice-start.6
  877.7 7.6 slice-start.7
  1137.0 17.2 %slice-start.15 = ((s8[5505024]{0:T(1024)(128)(4,1)}), s8[4194304]{0:T(1024)(128)(4,1)S(1)}, s32[]{:S(2)}) async-start(s8[5505024]{0:T(1024)(128)(4,1)} %bitcast.369), calls=%async_computation.32 | async-start | bytes 8388608
  1137.0 17.2 %slice-start.17 = ((s8[5505024]{0:T(1024)(128)(4,1)}), s8[4194304]{0:T(1024)(128)(4,1)S(1)}, s32[]{:S(2)}) async-start(s8[5505024]{0:T(1024)(128)(4,1)} %bitcast.371), calls=%async_computation.34 | async-start | bytes 8388608
  1142.3 12.0 slice-start.16
  1142.3 12.0 slice-start.18
  1176.6 23.3 %slice-start.4 = ((s8[5505024]{0:T(1024)(128)(4,1)}), s8[1310720]{0:T(1024)(128)(4,1)S(1)}, s32[]{:S(2)}) async-start(s8[5505024]{0:T(1024)(128)(4,1)} %bitcast.351), calls=%async_computation.21 | async-start | bytes 2621440
  1182.8 17.2 %slice-start.5 = ((s8[5505024]{0:T(1024)(128)(4,1)}), s8[4194304]{0:T(1024)(128)(4,1)S(1)}, s32[]{:S(2)}) async-start(s8[5505024]{0:T(1024)(128)(4,1)} %bitcast.351), calls=%async_computation.22 | async-start | bytes 8388608
  1200.0 12.6 %copy-start.13 = (bf16[1024,2048]{1,0:T(8,128)(2,1)S(1)}, bf16[1024,2048]{1,0:T(8,128)(2,1)}, u32[]{:S(2)}) copy-start(bf16[1024,2048]{1,0:T(8,128)(2,1)} %all-gather.10.cloned.1.call-done) | copy-start | bytes 12582916
  (22 other events, 69.1 us)
Sparse Core Ops, SparseCore 0:
  12.0 217.6 all-gather.5
  340.6 44.4 reduce-scatter.8
  388.8 34.4 all-gather.7
  508.6 44.5 reduce-scatter.12
  556.2 44.4 reduce-scatter.10
  735.7 44.4 reduce-scatter.14
  781.8 34.4 all-gather.9
  819.8 63.4 reduce-scatter.18
  884.9 33.4 all-gather.11
  920.8 216.2 reduce-scatter.16
